TPU v7x, 32 devices: a whole 2x2x4 slice. The times are simulated.
32 devices in a mesh: group: 8 (over y, x, core), seq: 4 (over z).
Axes of the slice: x: 2, y: 2, z: 4, core: 2. Of those that a mesh axis runs over, the one named last changes fastest.
Arguments:
- latent: float32 [16, 1024, 64], P('group', 'seq'), may hold values from -6 to 6
- margin_len: int32 [15], replicated, may hold values from 1 to 512, 5760 in all
- in_weight: bfloat16 [64, 1536], replicated, may hold values from -0.75 to 0.75
- norm_gain: float32 [1536], replicated, may hold values from 0.1 to 1.9
- qkv_weight: bfloat16 [3, 1536, 1024], P(None, None, 'seq'), may hold values from -0.15625 to 0.15625
- out_weight: bfloat16 [1024, 1536], P('seq'), may hold values from -0.1875 to 0.1875
- final_gain: float32 [1536], replicated, may hold values from 0.1 to 1.9
- head_out: bfloat16 [1536, 64], replicated, may hold values from -0.15625 to 0.15625
Outputs:
- next_latent: float32 [16, 1024, 64], P('group', 'seq')
Inputs may be any that keep to these rules, and one draw needn't show every extreme that they name: `margin_len`: the lengths sum to 15 * (384) and the largest is exactly 512.
All inputs are finite; a program needn't handle non-finite values.
Results may differ from a plain program's by a relative error of at most 0.0024.
Values may be sent and summed in bfloat16 or wider, within the bound.
No kernel may reach another device: no remote copies, remote signals or barrier semaphores. Data moves between devices by JAX's collectives and lax.ppermute only.
A program may use at most 128 MiB of HBM per device.

v0:
```python
import functools
import math

import jax
import jax.numpy as jnp
from jax import lax
from jax.experimental import pallas as pl
from jax.experimental.pallas import tpu as pltpu
from jax.sharding import PartitionSpec as P

HDIM = 64
OVMAX = 512
LANES = 128
QUAD = 4 * HDIM
STEP = -0.5
F32 = jnp.float32
BF16 = jnp.bfloat16
VMEM = pl.BlockSpec(memory_space=pltpu.VMEM)
SMEM = pl.BlockSpec(memory_space=pltpu.SMEM)


def limit(mebibytes):
    return pltpu.CompilerParams(vmem_limit_bytes=mebibytes << 20)


def iota(shape, dim):
    return lax.broadcasted_iota(jnp.int32, shape, dim)


def matmul(lhs, rhs):
    return jnp.dot(lhs, rhs, preferred_element_type=F32)


def matmul_nt(lhs, rhs, precision=None):
    return lax.dot_general(lhs, rhs, (((1,), (1,)), ((), ())), precision=precision, preferred_element_type=F32)


def split(value):
    high = value.astype(BF16)
    return high, (value - high.astype(F32)).astype(BF16)


def margin_at(margin_ref, index):
    last = margin_ref.shape[0]
    length = margin_ref[jnp.clip(index, 0, last - 1)]
    return jnp.where((index >= 0) & (index < last), length, 0)


def block_of(sub, shares):
    return lax.rem(sub, 2) * (shares // 2) + sub // 2


def started(pairs, sem):
    copies = [pltpu.make_async_copy(source, target, sem.at[i]) for i, (source, target) in enumerate(pairs)]
    for copy in copies:
        copy.start()
    return copies


def folded(both, weights, channels):
    product = matmul(both, weights)
    return product[:channels] + product[channels:]


def halves(value):
    channels = value.shape[1]
    value = jnp.concatenate([value, value], axis=1)
    high, low = split(value)
    left = iota(value.shape, 1) < channels
    return jnp.where(left, high.astype(F32), low.astype(F32)).astype(BF16)


def centered_rows(in_ref):
    weight = in_ref[...].astype(F32)
    return weight - jnp.mean(weight, axis=-1, keepdims=True)


def fold_kernel(shares, in_hbm, gain_hbm, qkv_hbm, out_hbm, final_hbm, head_hbm, *refs):
    map_ref, back_ref, part_ref, direct_ref, gram_ref = refs[:5]
    in_ref, gain_ref, qkv_ref, out_ref, final_ref, head_ref, sem = refs[5:]
    pairs = [(in_hbm, in_ref), (gain_hbm, gain_ref), (qkv_hbm.at[2], qkv_ref.at[2]), (out_hbm, out_ref)]
    pairs += [(qkv_hbm.at[0], qkv_ref.at[0]), (qkv_hbm.at[1], qkv_ref.at[1])]
    copies = started(pairs + [(final_hbm, final_ref), (head_hbm, head_ref)], sem)
    copies[0].wait()
    copies[1].wait()
    centered = centered_rows(in_ref)
    channels, depth = centered.shape
    width = out_ref.shape[0]
    both = jnp.concatenate(split(centered * gain_ref[...][None, :]), axis=0)

    high, low = split(centered)
    direct_ref[:channels, :depth] = high
    direct_ref[channels:, :depth] = low
    gram = matmul_nt(jnp.concatenate([high, low], axis=0), jnp.concatenate([high, low], axis=0))
    gram = (gram[:channels] + gram[channels:]) * (1.0 / depth)
    gram = gram + pltpu.roll(gram, channels, 1)
    first, _ = split(gram)
    second, third = split(gram - first.astype(F32))
    left = iota((channels, LANES), 1) < channels
    gram_ref[:, :LANES] = jnp.where(left, first.astype(F32), second.astype(F32)).astype(BF16)
    gram_ref[:, LANES:] = jnp.where(left, third.astype(F32), 0.0).astype(BF16)

    copies[2].wait()
    values = folded(both, qkv_ref[2], channels)
    tiled = jnp.concatenate([values] * (width // HDIM), axis=0)
    same = iota((width, width), 0) // channels == iota((width, width), 1) // HDIM
    high, low = split(jnp.where(same, tiled, 0.0))
    copies[3].wait()
    back = matmul(high, out_ref[...]) + matmul(low, out_ref[...])
    back = back - jnp.mean(back, axis=-1, keepdims=True)
    back_ref[:, :depth] = back.astype(BF16)
    copies[4].wait()
    queries = folded(both, qkv_ref[0], channels)
    copies[5].wait()
    keys = folded(both, qkv_ref[1], channels)
    map_ref[...] = jnp.concatenate([queries, keys], axis=0).T.astype(BF16)

    copies[6].wait()
    copies[7].wait()
    pieces = split(back * final_ref[...][None, :]) + split(centered * final_ref[...][None, :])
    scores = matmul_nt(jnp.concatenate(pieces, axis=0), head_ref[...])
    back_ref[:, depth:] = halves(scores[:width] + scores[width : 2 * width])
    direct_ref[:channels, depth:] = halves(scores[2 * width : 2 * width + channels] + scores[2 * width + channels :])
    direct_ref[channels:, depth:] = jnp.zeros((channels, LANES), BF16)
    rows = width // shares
    sub = lax.rem(lax.axis_index("group"), shares)
    part_ref[...] = back_ref[pl.ds(pl.multiple_of(block_of(sub, shares) * rows, rows), rows), :]


def twice(tokens):
    tokens = tokens.astype(F32)
    return tokens + pltpu.roll(tokens, LANES // 2, 1)


def bend(tokens, doubled, gram_ref):
    bent = matmul(tokens[:, : gram_ref.shape[0]], gram_ref[...])
    return (bent[:, :LANES] + bent[:, LANES:]) * doubled


def variance(bent):
    return jnp.maximum(jnp.sum(bent, axis=-1, keepdims=True), 0.0) + 1e-05


def quads(maps, mine, query_eps, key_eps, right_ref, ext_ref, sum_ref, key_scr, query_scr, p_scr):
    heads_width = maps.shape[0]
    total = right_ref.shape[0]
    share = mine.shape[0]
    channels = LANES // 2
    tile = min(total, 256)
    for start in range(0, total, tile):
        keys = matmul_nt(maps, right_ref[start : start + tile]).reshape(heads_width // HDIM, HDIM, tile)
        norm = jnp.mean(keys * keys, axis=1, keepdims=True)
        keys = keys * lax.rsqrt(norm + key_eps[None, :, start : start + tile])
        key_scr[:, start : start + tile] = keys.reshape(heads_width, tile).astype(BF16)
    one_head = iota((QUAD, QUAD), 0) // HDIM == iota((QUAD, QUAD), 1) // HDIM
    spread = jnp.where(one_head, 1.0 / HDIM, 0.0).astype(BF16)
    head_of = iota((share, QUAD), 1) // HDIM
    scale = HDIM ** (-0.5) * math.log2(math.e)
    left = iota((share, LANES), 1) < channels
    for quad in range(heads_width // QUAD):
        span = slice(quad * QUAD, (quad + 1) * QUAD)
        queries = matmul_nt(mine, maps[span, :])
        norm = matmul((queries * queries).astype(BF16), spread)
        queries = (queries * lax.rsqrt(norm + query_eps)).astype(BF16)
        for head in range(4):
            query_scr[quad % 2, head * share : (head + 1) * share, :] = jnp.where(
                head_of == head, queries, jnp.zeros_like(queries)
            )
        for start in range(0, total, tile):
            scores = matmul(query_scr[quad % 2], key_scr[span, start : start + tile])
            p_scr[quad % 2, :, start : start + tile] = jnp.exp2(scores * scale).astype(BF16)
        summed = matmul(p_scr[quad % 2], ext_ref[...])
        summed = summed[:, :LANES] / summed[:, LANES:]
        for pair in range(2):
            even = summed[2 * pair * share : (2 * pair + 1) * share]
            odd = summed[(2 * pair + 1) * share : (2 * pair + 2) * share]
            at = slice(quad * QUAD + pair * LANES, quad * QUAD + (pair + 1) * LANES)
            sum_ref[:share, at] = jnp.where(left, even, pltpu.roll(odd, HDIM, 1)).astype(BF16)
            sum_ref[share:, at] = jnp.where(left, pltpu.roll(even, HDIM, 1), odd).astype(BF16)


def attend_own_kernel(count, window, own_width, margin_ref, *refs):
    piece_refs, refs = refs[:count], refs[count:]
    map_ref, gram_ref, refs = refs[0], refs[1], refs[2:]
    if window:
        next_ref, refs = refs[0], refs[1:]
    sum_ref, right_ref, mine_ref, ext_ref, eps_ref, slot_scr, next_scr, win_scr, key_scr, query_scr, p_scr = refs
    total = win_scr.shape[0]
    channels = gram_ref.shape[0]
    share = total // count
    low = total - OVMAX
    group_pos = lax.axis_index("group")
    seq_pos = lax.axis_index("seq")
    over_len = margin_at(margin_ref, 2 * group_pos + window)
    own = total - over_len

    next_scr[:OVMAX, :] = jnp.zeros((OVMAX, LANES), F32)
    for k in range(count):
        source = jnp.bitwise_xor(seq_pos, k) * share
        at = pl.ds(pl.multiple_of(source, share), share)
        after = pl.ds(pl.multiple_of(source + OVMAX, share), share)
        slot = piece_refs[k][...].astype(F32)
        slot_scr[at, :] = pltpu.roll(slot, channels, 1) if window else slot
        next_scr[after, :] = next_ref[k].astype(F32) if window else pltpu.roll(slot, channels, 1)
    left = iota((OVMAX, LANES), 1) < channels
    for start in range(0, total, OVMAX):
        rows = slot_scr[start : start + OVMAX, :]
        if start >= low:
            tail = next_scr[pl.ds(over_len + (start - low), OVMAX), :]
            rows = jnp.where(iota(rows.shape, 0) + start < own, rows, tail)
        win_scr[start : start + OVMAX, :] = jnp.where(left, rows, 0.0).astype(BF16)

    win = win_scr[...]
    mine = win_scr[pl.ds(pl.multiple_of(seq_pos * share, share), share), :]
    mine_ref[...] = mine
    mine_twice = twice(mine)
    sum_ref[:share, own_width:] = mine_twice.astype(BF16)
    sum_ref[share:, own_width:] = mine_twice.astype(BF16)
    query_eps = variance(bend(mine, mine_twice, gram_ref)) * 1e-06
    doubled = twice(win)
    bent = bend(win, doubled, gram_ref)
    ones = jnp.ones((16, LANES), BF16)
    key_eps = (jnp.maximum(matmul_nt(ones, bent.astype(BF16))[:8], 0.0) + 1e-05) * 1e-06
    eps_ref[...] = key_eps

    scaled = doubled * lax.rsqrt(variance(bent))
    counted = (iota((total, LANES), 0) >= jnp.minimum(own, total - 1)).astype(F32)
    left = iota((total, LANES), 1) < channels
    ext_ref[:, :LANES] = jnp.where(left, scaled, scaled * counted).astype(BF16)
    ext_ref[:, LANES:] = jnp.where(left, 1.0, counted).astype(BF16)
    right_ref[...] = jnp.where(left, 0.0, doubled).astype(BF16)
    if own_width:
        quads(map_ref[...], mine, query_eps, key_eps[:1], right_ref, ext_ref, sum_ref, key_scr, query_scr, p_scr)


def attend_rest_kernel(gram_ref, right_ref, mine_ref, ext_ref, eps_ref, *refs):
    map_refs, refs = refs[:-5], refs[-5:]
    sum_ref, map_scr, key_scr, query_scr, p_scr = refs
    width = map_refs[0].shape[0]
    for k, ref in enumerate(map_refs):
        map_scr[k * width : (k + 1) * width, :] = ref[...]
    mine = mine_ref[...]
    query_eps = variance(bend(mine, twice(mine), gram_ref)) * 1e-06
    maps = map_scr[...]
    quads(maps, mine, query_eps, eps_ref[:1, :], right_ref, ext_ref, sum_ref, key_scr, query_scr, p_scr)


def signed_rows(count, score, margin_ref, rows_ref, packed_first, packed_second):
    share = rows_ref.shape[1]
    total = share * count
    channels = LANES // 2
    group_pos = lax.axis_index("group")
    seq_pos = lax.axis_index("seq")
    position = iota((share, LANES), 0) + seq_pos * share
    left = iota((share // 2, LANES), 1) < channels
    for window, packed_ref in enumerate((packed_first, packed_second)):
        at = 2 * share * window
        own = total - margin_at(margin_ref, 2 * group_pos + window)
        margin = jnp.where(position >= own, score[at + share : at + 2 * share], 0.0)
        signed = score[at : at + share] - margin
        rows_ref[window] = signed
        packed_ref[...] = jnp.where(left, signed[: share // 2], signed[share // 2 :]).astype(BF16)


def finish_kernel(count, shares, high, margin_ref, *refs):
    first_ref, first_rest, second_ref, second_rest, direct_ref, back_ref, far_ref, near_ref = refs[:8]
    rows_ref, packed_first, packed_second, all_scr, square_scr = refs[8:]
    width = back_ref.shape[0]
    depth = back_ref.shape[1] - LANES
    full = width * count
    part = width // shares
    channels = direct_ref.shape[0] // 2
    group_pos = lax.axis_index("group")
    sub = lax.rem(group_pos, shares)
    all_scr[:width, :] = back_ref[...]
    all_scr[full:, :] = direct_ref[...]
    for i, m in enumerate(high):
        for near, ref in ((0, far_ref), (1, near_ref)):
            place = block_of(jnp.bitwise_xor(sub, m ^ near), shares) * part
            for k in range(1, count):
                all_scr[pl.ds(pl.multiple_of(place + k * width, part), part), :] = ref[i, k - 1]
    tile = 2 * LANES
    own = first_ref.shape[1] - LANES
    windows = ((first_ref, first_rest), (second_ref, second_rest))
    known = jnp.concatenate(
        [jnp.concatenate([ref[:, :own], rest[...], ref[:, own:]][not own :], axis=1) for ref, rest in windows], axis=0
    )
    for start in range(0, depth, tile):
        mixed = matmul(known, all_scr[:, start : start + tile])
        squares = mixed * mixed
        squares = squares[:, :LANES] + squares[:, LANES:]
        square_scr[...] = squares if start == 0 else square_scr[...] + squares
    score = matmul(known, all_scr[:, depth:])
    variance = jnp.sum(square_scr[...], axis=-1, keepdims=True) * (1.0 / depth)
    score = (score + pltpu.roll(score, channels, 1)) * lax.rsqrt(variance + 1e-05)
    signed_rows(count, score, margin_ref, rows_ref, packed_first, packed_second)


def half_known(rest_ref, count, core):
    width = rest_ref.shape[1] // (count - 1)
    half = width // 2
    starts = [pl.multiple_of(k * width + core * half, half) for k in range(count - 1)]
    return [rest_ref[:, pl.ds(start, half)] for start in starts]


def fill_half(all_scr, base, gathered_ref, sub, high, half, count):
    part = gathered_ref.shape[2]
    for i, m in enumerate(high):
        place = jnp.bitwise_xor(sub, m) // 2 * part
        for k in range(count - 1):
            all_scr[pl.ds(pl.multiple_of(base + k * half + place, part), part), :] = gathered_ref[i, k]


def finish_far_kernel(count, shares, high, *refs):
    first_ref, first_rest, second_ref, second_rest, direct_ref, back_ref, far_ref, sum_ref, all_scr = refs
    width = back_ref.shape[0]
    half = width // 2
    sub = lax.rem(lax.axis_index("group"), shares)
    core = lax.rem(sub, 2)
    all_scr[:width, :] = back_ref[...]
    fill_half(all_scr, width, far_ref, sub, high, half, count)
    all_scr[width + (count - 1) * half :, :] = direct_ref[...]
    windows = ((first_ref, first_rest), (second_ref, second_rest))
    known = jnp.concatenate(
        [
            jnp.concatenate([ref[:, :width], *half_known(rest, count, core), ref[:, width:]], axis=1)
            for ref, rest in windows
        ],
        axis=0,
    )
    columns = sum_ref.shape[1]
    for start in range(0, columns, 2 * LANES):
        at = slice(start, min(start + 2 * LANES, columns))
        sum_ref[:, at] = matmul(known, all_scr[:, at])


def finish_near_kernel(count, shares, high, margin_ref, *refs):
    first_rest, second_rest, near_ref, sum_ref, rows_ref, packed_first, packed_second, all_scr, square_scr = refs
    depth = sum_ref.shape[1] - LANES
    half = first_rest.shape[1] // (count - 1) // 2
    sub = jnp.bitwise_xor(lax.rem(lax.axis_index("group"), shares), 1)
    fill_half(all_scr, 0, near_ref, sub, high, half, count)
    core = lax.rem(sub, 2)
    known = jnp.concatenate(
        [jnp.concatenate(half_known(rest, count, core), axis=1) for rest in (first_rest, second_rest)], axis=0
    )
    for start in range(0, depth, 2 * LANES):
        at = slice(start, start + 2 * LANES)
        mixed = sum_ref[:, at] + matmul(known, all_scr[:, at])
        squares = mixed * mixed
        squares = squares[:, :LANES] + squares[:, LANES:]
        square_scr[...] = squares if start == 0 else square_scr[...] + squares
    score = sum_ref[:, depth:] + matmul(known, all_scr[:, depth:])
    variance_out = jnp.sum(square_scr[...], axis=-1, keepdims=True) * (1.0 / depth)
    score = (score + pltpu.roll(score, LANES // 2, 1)) * lax.rsqrt(variance_out + 1e-05)
    signed_rows(count, score, margin_ref, rows_ref, packed_first, packed_second)


def combine_kernel(count, deltas, margin_ref, latent_ref, rows_ref, *refs):
    out_ref, tail_scr = refs[2 * len(deltas) :]
    channels, share = latent_ref.shape[1:]
    total = share * count
    group_pos = lax.axis_index("group")
    seq_pos = lax.axis_index("seq")
    for slot in range(2):
        before = margin_at(margin_ref, 2 * group_pos + slot - 1)
        own = total - margin_at(margin_ref, 2 * group_pos + slot)
        tail_scr[...] = jnp.zeros_like(tail_scr)
        for delta, ref in zip(deltas, refs[slot * len(deltas) : (slot + 1) * len(deltas)]):
            row = (seq_pos + delta) * share - (total - OVMAX)
            for half in range(2):
                value = ref[...].astype(F32)
                value = pltpu.roll(value, channels, 1) if half else value
                at = pl.ds(pl.multiple_of(row + half * (share // 2), share // 2), share // 2)
                tail_scr[at, :] = value
        moved = tail_scr[pl.ds(OVMAX - before + seq_pos * share, share), :]
        score = (rows_ref[slot] + moved).T[:channels]
        keep = iota(score.shape, 1) + seq_pos * share < own
        out_ref[slot] = jnp.where(keep, latent_ref[slot] + STEP * score, 0.0)


def body(latent, margin_len, in_weight, norm_gain, qkv_weight, out_weight, final_gain, head_out):
    count = lax.axis_size("seq")
    groups = lax.axis_size("group")
    share, channels = latent.shape[1:]
    total = share * count
    width, depth = out_weight.shape
    full = width * count
    shares = min(groups, width // 16)
    high = range(0, shares, 2)

    def across(value, group_by, pairs):
        moves = [
            (g * count + i, (g + group_by) * count + j)
            for g in range(groups)
            for i, j in pairs
            if 0 <= g + group_by < groups
        ]
        return lax.ppermute(value, ("group", "seq"), moves)

    def swap(value, bits):
        return lax.ppermute(value, "group", [(g, g ^ bits) for g in range(groups)])

    def gathered(value):
        return [lax.ppermute(value, "seq", [(i, i ^ k) for i in range(count)]) for k in range(1, count)]

    turned = latent.transpose(0, 2, 1)
    packed = jnp.concatenate([latent[0], latent[1]], axis=1).astype(BF16)
    pieces = [packed] + gathered(packed)
    stacked = jnp.stack(pieces)
    following = across(stacked, -1, [(i, i) for i in range(count)])
    maps, back, part, direct, gram = pl.pallas_call(
        functools.partial(fold_kernel, shares),
        out_shape=(
            jax.ShapeDtypeStruct((width, LANES), BF16),
            jax.ShapeDtypeStruct((width, depth + LANES), BF16),
            jax.ShapeDtypeStruct((width // shares, depth + LANES), BF16),
            jax.ShapeDtypeStruct((2 * channels, depth + LANES), BF16),
            jax.ShapeDtypeStruct((channels, 2 * LANES), BF16),
        ),
        in_specs=[pl.BlockSpec(memory_space=pltpu.HBM)] * 6,
        compiler_params=limit(20),
        out_specs=(VMEM,) * 5,
        scratch_shapes=[
            pltpu.VMEM(in_weight.shape, BF16),
            pltpu.VMEM(norm_gain.shape, F32),
            pltpu.VMEM(qkv_weight.shape, BF16),
            pltpu.VMEM(out_weight.shape, BF16),
            pltpu.VMEM(final_gain.shape, F32),
            pltpu.VMEM(head_out.shape[::-1], BF16),
            pltpu.SemaphoreType.DMA((8,)),
        ],
        cost_estimate=pl.CostEstimate(flops=width * depth * 1200, bytes_accessed=8 * width * depth, transcendentals=0),
        name="fold",
    )(*[pltpu.with_memory_space_constraint(x, pltpu.HBM) for x in (in_weight, norm_gain, qkv_weight, out_weight, final_gain, head_out.T)])
    own_part = jnp.stack(gathered(part))
    far_maps = gathered(maps)
    own_width = width // QUAD * QUAD
    rest_maps = far_maps if own_width else [maps] + far_maps
    rest_width = full - own_width

    def attention(lanes):
        return pl.CostEstimate(
            flops=16 * share * total * lanes,
            bytes_accessed=4 * lanes * share,
            transcendentals=share * total * lanes // HDIM,
        )

    def scratch(lanes):
        return [
            pltpu.VMEM((lanes, total), BF16),
            pltpu.VMEM((2, 4 * share, QUAD), BF16),
            pltpu.VMEM((2, 4 * share, total), BF16),
        ]

    def attend_own(window):
        extra = [following] if window else []
        return pl.pallas_call(
            functools.partial(attend_own_kernel, count, window, own_width),
            out_shape=(
                jax.ShapeDtypeStruct((2 * share, own_width + LANES), BF16),
                jax.ShapeDtypeStruct((total, LANES), BF16),
                jax.ShapeDtypeStruct((share, LANES), BF16),
                jax.ShapeDtypeStruct((total, QUAD), BF16),
                jax.ShapeDtypeStruct((8, total), F32),
            ),
            in_specs=[SMEM] + [VMEM] * (count + len(extra) + 2),
            compiler_params=limit(24),
            out_specs=(VMEM,) * 5,
            scratch_shapes=[
                pltpu.VMEM((total, LANES), F32),
                pltpu.VMEM((OVMAX + total, LANES), F32),
                pltpu.VMEM((total, LANES), BF16),
                *scratch(max(own_width, QUAD)),
            ],
            cost_estimate=attention(max(own_width, QUAD)),
            name="attend_own",
        )(margin_len, *pieces, maps, gram, *extra)

    def attend_rest(state):
        return pl.pallas_call(
            attend_rest_kernel,
            out_shape=jax.ShapeDtypeStruct((2 * share, rest_width), BF16),
            in_specs=[VMEM] * (5 + len(rest_maps)),
            compiler_params=limit(28),
            out_specs=VMEM,
            scratch_shapes=[pltpu.VMEM((rest_width, LANES), BF16), *scratch(rest_width)],
            cost_estimate=attention(rest_width),
            name="attend_rest",
        )(gram, *state, *rest_maps)

    first, *first_state = attend_own(0)
    second, *second_state = attend_own(1)
    first_rest = attend_rest(first_state)
    second_rest = attend_rest(second_state)
    planes = [swap(own_part, bits) for bits in high[1:]]
    far = jnp.stack([own_part] + planes)
    near = swap(far, 1)
    scored = (
        jax.ShapeDtypeStruct((2, share, LANES), F32),
        jax.ShapeDtypeStruct((share // 2, LANES), BF16),
        jax.ShapeDtypeStruct((share // 2, LANES), BF16),
    )
    half = width // 2
    columns = depth + LANES
    if own_width == width and half % LANES == 0:
        near_rows = (count - 1) * half
        far_rows = width + near_rows + 2 * channels
        partial_sums = pl.pallas_call(
            functools.partial(finish_far_kernel, count, shares, list(high)),
            out_shape=jax.ShapeDtypeStruct((4 * share, columns), F32),
            in_specs=[VMEM] * 7,
            compiler_params=limit(24),
            out_specs=VMEM,
            scratch_shapes=[pltpu.VMEM((far_rows, columns), BF16)],
            cost_estimate=pl.CostEstimate(
                flops=8 * share * far_rows * columns, bytes_accessed=4 * columns * far_rows, transcendentals=0
            ),
            name="finish_far",
        )(first, first_rest, second, second_rest, direct, back, far)
        rows, *tails = pl.pallas_call(
            functools.partial(finish_near_kernel, count, shares, list(high)),
            out_shape=scored,
            in_specs=[SMEM] + [VMEM] * 4,
            compiler_params=limit(24),
            out_specs=(VMEM, VMEM, VMEM),
            scratch_shapes=[pltpu.VMEM((near_rows, columns), BF16), pltpu.VMEM((4 * share, LANES), F32)],
            cost_estimate=pl.CostEstimate(
                flops=8 * share * near_rows * columns, bytes_accessed=4 * columns * near_rows, transcendentals=0
            ),
            name="finish_near",
        )(margin_len, first_rest, second_rest, near, partial_sums)
    else:
        rows, *tails = pl.pallas_call(
            functools.partial(finish_kernel, count, shares, list(high)),
            out_shape=(
                jax.ShapeDtypeStruct((2, share, LANES), F32),
                jax.ShapeDtypeStruct((share // 2, LANES), BF16),
                jax.ShapeDtypeStruct((share // 2, LANES), BF16),
            ),
            in_specs=[SMEM] + [VMEM] * 8,
            compiler_params=limit(24),
            out_specs=(VMEM, VMEM, VMEM),
            scratch_shapes=[
                pltpu.VMEM((full + 2 * channels, depth + LANES), BF16),
                pltpu.VMEM((4 * share, LANES), F32),
            ],
            cost_estimate=pl.CostEstimate(
                flops=8 * share * full * depth, bytes_accessed=2 * full * depth, transcendentals=0
            ),
            name="finish",
        )(margin_len, first, first_rest, second, second_rest, direct, back, far, near)

    deltas = list(range((total - OVMAX) // share, count))
    received = []
    for window, group_by in ((1, 1), (0, 0)):
        received += [across(tails[window], group_by, [(i, i - d) for i in range(d, count)]) for d in deltas]
    turned = pl.pallas_call(
        functools.partial(combine_kernel, count, deltas),
        out_shape=jax.ShapeDtypeStruct(turned.shape, F32),
        in_specs=[SMEM] + [VMEM] * (2 + len(received)),
        compiler_params=limit(8),
        out_specs=VMEM,
        scratch_shapes=[pltpu.VMEM((OVMAX + total + share, LANES), F32)],
        name="combine",
    )(margin_len, turned, rows, *received)
    return turned.transpose(0, 2, 1)


def solution(mesh):
    in_specs = (
        P("group", "seq", None),
        P(),
        P(),
        P(),
        P(None, None, "seq"),
        P("seq", None),
        P(),
        P(),
    )
    out_specs = P("group", "seq", None)

    return jax.shard_map(body, mesh=mesh, in_specs=in_specs, out_specs=out_specs, check_vma=False)
```

profile of v0, /device:TPU:1, one launch (start us, length us, event | category | flops | bytes accessed | tf_op | source)
XLA Modules:
  0.0 85.8 jit_solution(16871966655698148716)
XLA Ops:
  0.0 4.2 %fold.1 = (bf16[256,128]{1,0:T(8,128)(2,1)S(1)}, bf16[256,1664]{1,0:T(8,128)(2,1)S(1)}, bf16[32,1664]{1,0:T(8,128)(2,1)S(1)}, bf16[128,1664]{1,0:T(8,128)(2,1)S(1)}, bf16[64,256]{1,0:T(8,128)(2,1)S(1)}) custom-call(bf16[64,1536]{1,0:T(8,128)(2,1)} %in_hbm.1, f32[1536]{0:T(1024)} %gain_hbm.1, bf16[3,1536,256]{2,1,0:T(8,128)(2,1)} %qkv_hbm.1, ...), custom_call_target="tpu_custom_call" | custom-call | flops 471859200 | bytes 3145728 | tf_op jit(solution)/shard_map/fold/pallas_call | solution.py:412
  4.2 2.2 %collective-permute-start.7 = (bf16[32,1664]{1,0:T(8,128)(2,1)S(1)}, bf16[32,1664]{1,0:T(8,128)(2,1)S(1)}, u32[]{:S(2)}, u32[]{:S(2)}) collective-permute-start(bf16[32,1664]{1,0:T(8,128)(2,1)S(1)} %get-tuple-element.33), channel_id=1, source_target_pairs={{0,1},{1,0},{2,3},{3,2},{4,5},{5,4},{6,7},{7,6},{8,9},{9,8},{10,11... | collective-permute-start | bytes 319496 | tf_op jit(solution)/shard_map/ppermute | solution.py:405
  6.4 2.3 %collective-permute-start.8 = (bf16[32,1664]{1,0:T(8,128)(2,1)S(1)}, bf16[32,1664]{1,0:T(8,128)(2,1)S(1)}, u32[]{:S(2)}, u32[]{:S(2)}) collective-permute-start(bf16[32,1664]{1,0:T(8,128)(2,1)S(1)} %get-tuple-element.33), channel_id=1, source_target_pairs={{0,2},{1,3},{2,0},{3,1},{4,6},{5,7},{6,4},{7,5},{8,10},{9,11},{10,... | collective-permute-start | bytes 319496 | tf_op jit(solution)/shard_map/ppermute | solution.py:405
  8.7 0.0 collective-permute-start.9
  8.7 0.4 collective-permute-done.7
  9.1 1.9 %collective-permute-done.8 = bf16[32,1664]{1,0:T(8,128)(2,1)S(1)} collective-permute-done((bf16[32,1664]{1,0:T(8,128)(2,1)S(1)}, bf16[32,1664]{1,0:T(8,128)(2,1)S(1)}, u32[]{:S(2)}, u32[]{:S(2)}) %collective-permute-start.8) | collective-permute-done | bytes 106528 | tf_op jit(solution)/shard_map/ppermute | solution.py:405
  11.0 4.6 %collective-permute-done.9 = bf16[32,1664]{1,0:T(8,128)(2,1)S(1)} collective-permute-done((bf16[32,1664]{1,0:T(8,128)(2,1)S(1)}, bf16[32,1664]{1,0:T(8,128)(2,1)S(1)}, u32[]{:S(2)}, u32[]{:S(2)}) %collective-permute-start.9) | collective-permute-done | bytes 106528 | tf_op jit(solution)/shard_map/ppermute | solution.py:405
  15.6 0.1 fusion
  15.6 1.2 %collective-permute-start.10 = (bf16[3,32,1664]{2,1,0:T(8,128)(2,1)S(1)}, bf16[3,32,1664]{2,1,0:T(8,128)(2,1)S(1)}, u32[]{:S(2)}, u32[]{:S(2)}) collective-permute-start(bf16[3,32,1664]{2,1,0:T(8,128)(2,1)S(1)} %get-tuple-element.42), channel_id=1, source_target_pairs={{0,8},{4,12},{8,0},{12,4},{16,24},{20,28},{24,16},{28,20},{1,9},{5... | collective-permute-start | bytes 958472 | tf_op jit(solution)/shard_map/ppermute | solution.py:402
  16.9 1.2 %collective-permute-start.11 = (bf16[3,32,1664]{2,1,0:T(8,128)(2,1)S(1)}, bf16[3,32,1664]{2,1,0:T(8,128)(2,1)S(1)}, u32[]{:S(2)}, u32[]{:S(2)}) collective-permute-start(bf16[3,32,1664]{2,1,0:T(8,128)(2,1)S(1)} %get-tuple-element.42), channel_id=1, source_target_pairs={{0,16},{4,20},{8,24},{12,28},{16,0},{20,4},{24,8},{28,12},{1,17},{... | collective-permute-start | bytes 958472 | tf_op jit(solution)/shard_map/ppermute | solution.py:402
  18.1 0.2 collective-permute-start.12
  18.4 0.1 copy.11
  18.5 0.1 copy.12
  18.6 3.4 %collective-permute-done.10 = bf16[3,32,1664]{2,1,0:T(8,128)(2,1)S(1)} collective-permute-done((bf16[3,32,1664]{2,1,0:T(8,128)(2,1)S(1)}, bf16[3,32,1664]{2,1,0:T(8,128)(2,1)S(1)}, u32[]{:S(2)}, u32[]{:S(2)}) %collective-permute-start.10) | collective-permute-done | bytes 319520 | tf_op jit(solution)/shard_map/ppermute | solution.py:402
  22.0 1.5 %collective-permute-done.11 = bf16[3,32,1664]{2,1,0:T(8,128)(2,1)S(1)} collective-permute-done((bf16[3,32,1664]{2,1,0:T(8,128)(2,1)S(1)}, bf16[3,32,1664]{2,1,0:T(8,128)(2,1)S(1)}, u32[]{:S(2)}, u32[]{:S(2)}) %collective-permute-start.11) | collective-permute-done | bytes 319520 | tf_op jit(solution)/shard_map/ppermute | solution.py:402
  23.5 6.2 %collective-permute-done.12 = bf16[3,32,1664]{2,1,0:T(8,128)(2,1)S(1)} collective-permute-done((bf16[3,32,1664]{2,1,0:T(8,128)(2,1)S(1)}, bf16[3,32,1664]{2,1,0:T(8,128)(2,1)S(1)}, u32[]{:S(2)}, u32[]{:S(2)}) %collective-permute-start.12) | collective-permute-done | bytes 319520 | tf_op jit(solution)/shard_map/ppermute | solution.py:402
  29.7 0.2 pad_maximum_fusion.refs_6_
  29.9 4.1 %collective-permute-start.13 = (bf16[4,3,32,1664]{3,2,1,0:T(8,128)(2,1)S(1)}, bf16[4,3,32,1664]{3,2,1,0:T(8,128)(2,1)S(1)}, u32[]{:S(2)}, u32[]{:S(2)}) collective-permute-start(bf16[4,3,32,1664]{3,2,1,0:T(8,128)(2,1)S(1)} %pad_maximum_fusion.refs_6_), channel_id=1, source_target_pairs={{0,4},{4,0},{8,12},{12,8},{16,20},{20,16},{24,28},{28,24},{1,5},{5... | collective-permute-start | bytes 3833864 | tf_op jit(solution)/shard_map/ppermute | solution.py:402
  34.0 0.1 pad_maximum_fusion.3.refs_0_
  34.1 2.5 %collective-permute-start = (bf16[256,128]{1,0:T(8,128)(2,1)S(1)}, bf16[256,128]{1,0:T(8,128)(2,1)S(1)}, u32[]{:S(2)}, u32[]{:S(2)}) collective-permute-start(bf16[256,128]{1,0:T(8,128)(2,1)S(1)} %pad_maximum_fusion.3.refs_0_), channel_id=1, source_target_pairs={{0,1},{1,0},{2,3},{3,2},{4,5},{5,4},{6,7},{7,6},{8,9},{9,8},{10,11... | collective-permute-start | bytes 196616 | tf_op jit(solution)/shard_map/ppermute | solution.py:405
  36.5 1.5 %collective-permute-start.1 = (bf16[256,128]{1,0:T(8,128)(2,1)S(1)}, bf16[256,128]{1,0:T(8,128)(2,1)S(1)}, u32[]{:S(2)}, u32[]{:S(2)}) collective-permute-start(bf16[256,128]{1,0:T(8,128)(2,1)S(1)} %pad_maximum_fusion.3.refs_0_), channel_id=1, source_target_pairs={{0,2},{1,3},{2,0},{3,1},{4,6},{5,7},{6,4},{7,5},{8,10},{9,11},{10,... | collective-permute-start | bytes 196616 | tf_op jit(solution)/shard_map/ppermute | solution.py:405
  38.0 1.1 %collective-permute-start.2 = (bf16[256,128]{1,0:T(8,128)(2,1)S(1)}, bf16[256,128]{1,0:T(8,128)(2,1)S(1)}, u32[]{:S(2)}, u32[]{:S(2)}) collective-permute-start(bf16[256,128]{1,0:T(8,128)(2,1)S(1)} %pad_maximum_fusion.3.refs_0_), channel_id=1, source_target_pairs={{0,3},{1,2},{2,1},{3,0},{4,7},{5,6},{6,5},{7,4},{8,11},{9,10},{10,... | collective-permute-start | bytes 196616 | tf_op jit(solution)/shard_map/ppermute | solution.py:405
  39.1 0.3 collective-permute-start.3
  39.4 0.0 collective-permute-done.refs_1_
  39.4 2.2 %collective-permute-start.4 = (bf16[256,128]{1,0:T(8,128)(2,1)S(1)}, bf16[256,128]{1,0:T(8,128)(2,1)S(1)}, u32[]{:S(2)}, u32[]{:S(2)}) collective-permute-start(bf16[256,128]{1,0:T(8,128)(2,1)S(1)} %get-tuple-element.24.refs_4_), channel_id=1, source_target_pairs={{0,2},{1,3},{2,0},{3,1},{4,6},{5,7},{6,4},{7,5},{8,10},{9,11},{10,... | collective-permute-start | bytes 196616 | tf_op jit(solution)/shard_map/ppermute | solution.py:405
  41.6 0.0 collective-permute-done.1.refs_2_
  41.6 5.5 %collective-permute-start.5 = (bf16[256,128]{1,0:T(8,128)(2,1)S(1)}, bf16[256,128]{1,0:T(8,128)(2,1)S(1)}, u32[]{:S(2)}, u32[]{:S(2)}) collective-permute-start(bf16[256,128]{1,0:T(8,128)(2,1)S(1)} %get-tuple-element.24.refs_4_), channel_id=1, source_target_pairs={{0,3},{1,2},{2,1},{3,0},{4,7},{5,6},{6,5},{7,4},{8,11},{9,10},{10,... | collective-permute-start | bytes 196616 | tf_op jit(solution)/shard_map/ppermute | solution.py:405
  47.1 0.0 collective-permute-done.2.refs_3_
  47.1 0.1 pad_maximum_fusion.2
  47.2 3.0 %collective-permute-start.6 = (bf16[4,256,128]{2,1,0:T(8,128)(2,1)S(1)}, bf16[4,256,128]{2,1,0:T(8,128)(2,1)S(1)}, u32[]{:S(2)}, u32[]{:S(2)}) collective-permute-start(bf16[4,256,128]{2,1,0:T(8,128)(2,1)S(1)} %pad_maximum_fusion.2), channel_id=1, source_target_pairs={{4,0},{5,1},{6,2},{7,3},{8,4},{9,5},{10,6},{11,7},{12,8},{13,9},{1... | collective-permute-start | bytes 786440 | tf_op jit(solution)/shard_map/ppermute | solution.py:399
  50.2 3.2 %attend_own.2 = (bf16[512,384]{1,0:T(8,128)(2,1)S(1)}, bf16[1024,128]{1,0:T(8,128)(2,1)S(1)}, bf16[256,128]{1,0:T(8,128)(2,1)S(1)}, bf16[1024,256]{1,0:T(8,128)(2,1)S(1)}, f32[8,1024]{1,0:T(8,128)S(1)}) custom-call(s32[15]{0:T(128)S(1)} %copy-done.1, bf16[256,128]{1,0:T(8,128)(2,1)S(1)} %pad_maximum_fusion.3.refs_0_, ...), custom_call_target="tpu_custom_call" | custom-call | flops 1073741824 | bytes 262144 | tf_op jit(solution)/shard_map/attend_own/pallas_call | solution.py:458
  53.4 0.0 collective-permute-done.3.refs_0_
  53.4 0.0 collective-permute-done.5.refs_2_
  53.4 4.9 %attend_rest.2.refs_1_.refs_0_ = bf16[512,768]{1,0:T(8,128)(2,1)S(1)} custom-call(bf16[64,256]{1,0:T(8,128)(2,1)S(1)} %get-tuple-element.23.refs_5_.gram_ref, bf16[1024,128]{1,0:T(8,128)(2,1)S(1)} %get-tuple-element.25.right_ref, bf16[256,128]{1,0:T(8,128)(2,1)S(1)} %get-tuple-element.26.mine_ref, bf16[1024,256]{1,0:T(8,128)(2,1)S(1)} %get-tuple-element.27.ext_ref, ...), custom_call_target="tpu_custom_call" | custom-call | flops 3221225472 | bytes 786432 | tf_op jit(solution)/shard_map/attend_rest/pallas_call | solution.py:481
  58.3 0.0 collective-permute-done.6.refs_6_
  58.3 3.2 %attend_own.3 = (bf16[512,384]{1,0:T(8,128)(2,1)S(1)}, bf16[1024,128]{1,0:T(8,128)(2,1)S(1)}, bf16[256,128]{1,0:T(8,128)(2,1)S(1)}, bf16[1024,256]{1,0:T(8,128)(2,1)S(1)}, f32[8,1024]{1,0:T(8,128)S(1)}) custom-call(s32[15]{0:T(128)S(1)} %copy-done.1, bf16[256,128]{1,0:T(8,128)(2,1)S(1)} %pad_maximum_fusion.3.refs_0_, ...), custom_call_target="tpu_custom_call" | custom-call | flops 1073741824 | bytes 262144 | tf_op jit(solution)/shard_map/attend_own/pallas_call | solution.py:458
  61.5 5.1 %attend_rest.3.refs_3_.refs_1_ = bf16[512,768]{1,0:T(8,128)(2,1)S(1)} custom-call(bf16[64,256]{1,0:T(8,128)(2,1)S(1)} %get-tuple-element.23.refs_5_.gram_ref, bf16[1024,128]{1,0:T(8,128)(2,1)S(1)} %get-tuple-element.29.right_ref, bf16[256,128]{1,0:T(8,128)(2,1)S(1)} %get-tuple-element.30.mine_ref, bf16[1024,256]{1,0:T(8,128)(2,1)S(1)} %get-tuple-element.31.ext_ref, ...), custom_call_target="tpu_custom_call" | custom-call | flops 3221225472 | bytes 786432 | tf_op jit(solution)/shard_map/attend_rest/pallas_call | solution.py:481
  66.7 3.2 %finish_far.1.refs_3_ = f32[1024,1664]{1,0:T(8,128)S(1)} custom-call(bf16[512,384]{1,0:T(8,128)(2,1)S(1)} %get-tuple-element.34.refs_0_, bf16[512,768]{1,0:T(8,128)(2,1)S(1)} %attend_rest.2.refs_1_.refs_0_, bf16[512,384]{1,0:T(8,128)(2,1)S(1)} %get-tuple-element.35.refs_2_, bf16[512,768]{1,0:T(8,128)(2,1)S(1)} %attend_rest.3.refs_3_.refs_1_, ...), custom_call_target="tpu_custom_call" | custom-call | flops 2617245696 | bytes 5111808 | tf_op jit(solution)/shard_map/finish_far/pallas_call | solution.py:509
  69.9 2.9 %finish_near.1 = (f32[2,256,128]{2,1,0:T(8,128)S(1)}, bf16[128,128]{1,0:T(8,128)(2,1)S(1)}, bf16[128,128]{1,0:T(8,128)(2,1)S(1)}) custom-call(s32[15]{0:T(128)S(1)} %copy-done.1, bf16[512,768]{1,0:T(8,128)(2,1)S(1)} %attend_rest.2.refs_1_.refs_0_, bf16[512,768]{1,0:T(8,128)(2,1)S(1)} %attend_rest.3.refs_3_.refs_1_, ...), custom_call_target="tpu_custom_call" | custom-call | flops 1308622848 | bytes 2555904 | tf_op jit(solution)/shard_map/finish_near/pallas_call | solution.py:521
  72.8 1.3 %collective-permute-start.14 = (bf16[128,128]{1,0:T(8,128)(2,1)S(1)}, bf16[128,128]{1,0:T(8,128)(2,1)S(1)}, u32[]{:S(2)}, u32[]{:S(2)}) collective-permute-start(bf16[128,128]{1,0:T(8,128)(2,1)S(1)} %get-tuple-element.39), channel_id=1, source_target_pairs={{2,4},{3,5},{6,8},{7,9},{10,12},{11,13},{14,16},{15,17},{18,20},{1... | collective-permute-start | bytes 98312 | tf_op jit(solution)/shard_map/ppermute | solution.py:399
  74.1 1.3 %collective-permute-start.15 = (bf16[128,128]{1,0:T(8,128)(2,1)S(1)}, bf16[128,128]{1,0:T(8,128)(2,1)S(1)}, u32[]{:S(2)}, u32[]{:S(2)}) collective-permute-start(bf16[128,128]{1,0:T(8,128)(2,1)S(1)} %get-tuple-element.39), channel_id=1, source_target_pairs={{3,4},{7,8},{11,12},{15,16},{19,20},{23,24},{27,28}} | collective-permute-start | bytes 98312 | tf_op jit(solution)/shard_map/ppermute | solution.py:399
  75.4 1.3 %collective-permute-start.16 = (bf16[128,128]{1,0:T(8,128)(2,1)S(1)}, bf16[128,128]{1,0:T(8,128)(2,1)S(1)}, u32[]{:S(2)}, u32[]{:S(2)}) collective-permute-start(bf16[128,128]{1,0:T(8,128)(2,1)S(1)} %get-tuple-element.40), channel_id=1, source_target_pairs={{2,0},{3,1},{6,4},{7,5},{10,8},{11,9},{14,12},{15,13},{18,16},{19,... | collective-permute-start | bytes 98312 | tf_op jit(solution)/shard_map/ppermute | solution.py:399
  76.7 1.3 %collective-permute-start.17 = (bf16[128,128]{1,0:T(8,128)(2,1)S(1)}, bf16[128,128]{1,0:T(8,128)(2,1)S(1)}, u32[]{:S(2)}, u32[]{:S(2)}) collective-permute-start(bf16[128,128]{1,0:T(8,128)(2,1)S(1)} %get-tuple-element.40), channel_id=1, source_target_pairs={{3,0},{7,4},{11,8},{15,12},{19,16},{23,20},{27,24},{31,28}} | collective-permute-start | bytes 98312 | tf_op jit(solution)/shard_map/ppermute | solution.py:399
  78.0 1.3 %collective-permute-done.14.refs_0_ = bf16[128,128]{1,0:T(8,128)(2,1)S(1)} collective-permute-done((bf16[128,128]{1,0:T(8,128)(2,1)S(1)}, bf16[128,128]{1,0:T(8,128)(2,1)S(1)}, u32[]{:S(2)}, u32[]{:S(2)}) %collective-permute-start.14) | collective-permute-done | bytes 32800 | tf_op jit(solution)/shard_map/ppermute | solution.py:399
  79.3 2.3 %collective-permute-done.15.refs_1_ = bf16[128,128]{1,0:T(8,128)(2,1)S(1)} collective-permute-done((bf16[128,128]{1,0:T(8,128)(2,1)S(1)}, bf16[128,128]{1,0:T(8,128)(2,1)S(1)}, u32[]{:S(2)}, u32[]{:S(2)}) %collective-permute-start.15) | collective-permute-done | bytes 32800 | tf_op jit(solution)/shard_map/ppermute | solution.py:399
  81.6 0.6 collective-permute-done.16.refs_2_
  82.2 2.2 %collective-permute-done.17.refs_3_ = bf16[128,128]{1,0:T(8,128)(2,1)S(1)} collective-permute-done((bf16[128,128]{1,0:T(8,128)(2,1)S(1)}, bf16[128,128]{1,0:T(8,128)(2,1)S(1)}, u32[]{:S(2)}, u32[]{:S(2)}) %collective-permute-start.17) | collective-permute-done | bytes 32800 | tf_op jit(solution)/shard_map/ppermute | solution.py:399
  84.4 1.5 %combine.1 = f32[2,64,256]{2,1,0:T(8,128)} custom-call(s32[15]{0:T(128)S(1)} %copy-done.1, f32[2,64,256]{2,1,0:T(8,128)S(1)} %bitcast.16, f32[2,256,128]{2,1,0:T(8,128)S(1)} %get-tuple-element.38.rows_ref, bf16[128,128]{1,0:T(8,128)(2,1)S(1)} %collective-permute-done.14.refs_0_, bf16[128,128]{1,0:T(8,128)(2,1)S(1)} %collective-permute-done.15.refs_1_, ...), custom_call_target="tpu_custom_call" | custom-call | tf_op jit(solution)/shard_map/combine/pallas_call | solution.py:558
  (7 shorter events, 0.0 us)
Async XLA Ops:
  0.0 18.4 %copy-start = (f32[2,256,64]{1,2,0:T(8,128)S(1)}, f32[2,256,64]{1,2,0:T(8,128)}, u32[]{:S(2)}) copy-start(f32[2,256,64]{1,2,0:T(8,128)} %param.8) | copy-start | bytes 393220
  4.2 4.9 %collective-permute-start.7 = (bf16[32,1664]{1,0:T(8,128)(2,1)S(1)}, bf16[32,1664]{1,0:T(8,128)(2,1)S(1)}, u32[]{:S(2)}, u32[]{:S(2)}) collective-permute-start(bf16[32,1664]{1,0:T(8,128)(2,1)S(1)} %get-tuple-element.33), channel_id=1, source_target_pairs={{0,1},{1,0},{2,3},{3,2},{4,5},{5,4},{6,7},{7,6},{8,9},{9,8},{10,11... | collective-permute-start | bytes 319496 | tf_op jit(solution)/shard_map/ppermute | solution.py:405
  6.4 4.6 %collective-permute-start.8 = (bf16[32,1664]{1,0:T(8,128)(2,1)S(1)}, bf16[32,1664]{1,0:T(8,128)(2,1)S(1)}, u32[]{:S(2)}, u32[]{:S(2)}) collective-permute-start(bf16[32,1664]{1,0:T(8,128)(2,1)S(1)} %get-tuple-element.33), channel_id=1, source_target_pairs={{0,2},{1,3},{2,0},{3,1},{4,6},{5,7},{6,4},{7,5},{8,10},{9,11},{10,... | collective-permute-start | bytes 319496 | tf_op jit(solution)/shard_map/ppermute | solution.py:405
  8.7 6.9 %collective-permute-start.9 = (bf16[32,1664]{1,0:T(8,128)(2,1)S(1)}, bf16[32,1664]{1,0:T(8,128)(2,1)S(1)}, u32[]{:S(2)}, u32[]{:S(2)}) collective-permute-start(bf16[32,1664]{1,0:T(8,128)(2,1)S(1)} %get-tuple-element.33), channel_id=1, source_target_pairs={{0,3},{1,2},{2,1},{3,0},{4,7},{5,6},{6,5},{7,4},{8,11},{9,10},{10,... | collective-permute-start | bytes 319496 | tf_op jit(solution)/shard_map/ppermute | solution.py:405
  15.6 6.4 %collective-permute-start.10 = (bf16[3,32,1664]{2,1,0:T(8,128)(2,1)S(1)}, bf16[3,32,1664]{2,1,0:T(8,128)(2,1)S(1)}, u32[]{:S(2)}, u32[]{:S(2)}) collective-permute-start(bf16[3,32,1664]{2,1,0:T(8,128)(2,1)S(1)} %get-tuple-element.42), channel_id=1, source_target_pairs={{0,8},{4,12},{8,0},{12,4},{16,24},{20,28},{24,16},{28,20},{1,9},{5... | collective-permute-start | bytes 958472 | tf_op jit(solution)/shard_map/ppermute | solution.py:402
  16.9 6.6 %collective-permute-start.11 = (bf16[3,32,1664]{2,1,0:T(8,128)(2,1)S(1)}, bf16[3,32,1664]{2,1,0:T(8,128)(2,1)S(1)}, u32[]{:S(2)}, u32[]{:S(2)}) collective-permute-start(bf16[3,32,1664]{2,1,0:T(8,128)(2,1)S(1)} %get-tuple-element.42), channel_id=1, source_target_pairs={{0,16},{4,20},{8,24},{12,28},{16,0},{20,4},{24,8},{28,12},{1,17},{... | collective-permute-start | bytes 958472 | tf_op jit(solution)/shard_map/ppermute | solution.py:402
  18.1 11.6 %collective-permute-start.12 = (bf16[3,32,1664]{2,1,0:T(8,128)(2,1)S(1)}, bf16[3,32,1664]{2,1,0:T(8,128)(2,1)S(1)}, u32[]{:S(2)}, u32[]{:S(2)}) collective-permute-start(bf16[3,32,1664]{2,1,0:T(8,128)(2,1)S(1)} %get-tuple-element.42), channel_id=1, source_target_pairs={{0,24},{4,28},{8,16},{12,20},{16,8},{20,12},{24,0},{28,4},{1,25},{... | collective-permute-start | bytes 958472 | tf_op jit(solution)/shard_map/ppermute | solution.py:402
  29.7 20.5 %copy-start.1 = (s32[15]{0:T(128)S(1)}, s32[15]{0:T(128)}, u32[]{:S(2)}) copy-start(s32[15]{0:T(128)} %margin_ref.7) | copy-start | bytes 184
  29.9 40.0 %collective-permute-start.13 = (bf16[4,3,32,1664]{3,2,1,0:T(8,128)(2,1)S(1)}, bf16[4,3,32,1664]{3,2,1,0:T(8,128)(2,1)S(1)}, u32[]{:S(2)}, u32[]{:S(2)}) collective-permute-start(bf16[4,3,32,1664]{3,2,1,0:T(8,128)(2,1)S(1)} %pad_maximum_fusion.refs_6_), channel_id=1, source_target_pairs={{0,4},{4,0},{8,12},{12,8},{16,20},{20,16},{24,28},{28,24},{1,5},{5... | collective-permute-start | bytes 3833864 | tf_op jit(solution)/shard_map/ppermute | solution.py:402
  34.1 5.4 %collective-permute-start = (bf16[256,128]{1,0:T(8,128)(2,1)S(1)}, bf16[256,128]{1,0:T(8,128)(2,1)S(1)}, u32[]{:S(2)}, u32[]{:S(2)}) collective-permute-start(bf16[256,128]{1,0:T(8,128)(2,1)S(1)} %pad_maximum_fusion.3.refs_0_), channel_id=1, source_target_pairs={{0,1},{1,0},{2,3},{3,2},{4,5},{5,4},{6,7},{7,6},{8,9},{9,8},{10,11... | collective-permute-start | bytes 196616 | tf_op jit(solution)/shard_map/ppermute | solution.py:405
  36.5 5.1 %collective-permute-start.1 = (bf16[256,128]{1,0:T(8,128)(2,1)S(1)}, bf16[256,128]{1,0:T(8,128)(2,1)S(1)}, u32[]{:S(2)}, u32[]{:S(2)}) collective-permute-start(bf16[256,128]{1,0:T(8,128)(2,1)S(1)} %pad_maximum_fusion.3.refs_0_), channel_id=1, source_target_pairs={{0,2},{1,3},{2,0},{3,1},{4,6},{5,7},{6,4},{7,5},{8,10},{9,11},{10,... | collective-permute-start | bytes 196616 | tf_op jit(solution)/shard_map/ppermute | solution.py:405
  38.0 9.1 %collective-permute-start.2 = (bf16[256,128]{1,0:T(8,128)(2,1)S(1)}, bf16[256,128]{1,0:T(8,128)(2,1)S(1)}, u32[]{:S(2)}, u32[]{:S(2)}) collective-permute-start(bf16[256,128]{1,0:T(8,128)(2,1)S(1)} %pad_maximum_fusion.3.refs_0_), channel_id=1, source_target_pairs={{0,3},{1,2},{2,1},{3,0},{4,7},{5,6},{6,5},{7,4},{8,11},{9,10},{10,... | collective-permute-start | bytes 196616 | tf_op jit(solution)/shard_map/ppermute | solution.py:405
  39.1 14.2 %collective-permute-start.3 = (bf16[256,128]{1,0:T(8,128)(2,1)S(1)}, bf16[256,128]{1,0:T(8,128)(2,1)S(1)}, u32[]{:S(2)}, u32[]{:S(2)}) collective-permute-start(bf16[256,128]{1,0:T(8,128)(2,1)S(1)} %get-tuple-element.24.refs_4_), channel_id=1, source_target_pairs={{0,1},{1,0},{2,3},{3,2},{4,5},{5,4},{6,7},{7,6},{8,9},{9,8},{10,11... | collective-permute-start | bytes 196616 | tf_op jit(solution)/shard_map/ppermute | solution.py:405
  39.4 14.0 %collective-permute-start.4 = (bf16[256,128]{1,0:T(8,128)(2,1)S(1)}, bf16[256,128]{1,0:T(8,128)(2,1)S(1)}, u32[]{:S(2)}, u32[]{:S(2)}) collective-permute-start(bf16[256,128]{1,0:T(8,128)(2,1)S(1)} %get-tuple-element.24.refs_4_), channel_id=1, source_target_pairs={{0,2},{1,3},{2,0},{3,1},{4,6},{5,7},{6,4},{7,5},{8,10},{9,11},{10,... | collective-permute-start | bytes 196616 | tf_op jit(solution)/shard_map/ppermute | solution.py:405
  41.6 11.8 %collective-permute-start.5 = (bf16[256,128]{1,0:T(8,128)(2,1)S(1)}, bf16[256,128]{1,0:T(8,128)(2,1)S(1)}, u32[]{:S(2)}, u32[]{:S(2)}) collective-permute-start(bf16[256,128]{1,0:T(8,128)(2,1)S(1)} %get-tuple-element.24.refs_4_), channel_id=1, source_target_pairs={{0,3},{1,2},{2,1},{3,0},{4,7},{5,6},{6,5},{7,4},{8,11},{9,10},{10,... | collective-permute-start | bytes 196616 | tf_op jit(solution)/shard_map/ppermute | solution.py:405
  47.2 11.1 %collective-permute-start.6 = (bf16[4,256,128]{2,1,0:T(8,128)(2,1)S(1)}, bf16[4,256,128]{2,1,0:T(8,128)(2,1)S(1)}, u32[]{:S(2)}, u32[]{:S(2)}) collective-permute-start(bf16[4,256,128]{2,1,0:T(8,128)(2,1)S(1)} %pad_maximum_fusion.2), channel_id=1, source_target_pairs={{4,0},{5,1},{6,2},{7,3},{8,4},{9,5},{10,6},{11,7},{12,8},{13,9},{1... | collective-permute-start | bytes 786440 | tf_op jit(solution)/shard_map/ppermute | solution.py:399
  72.8 6.5 %collective-permute-start.14 = (bf16[128,128]{1,0:T(8,128)(2,1)S(1)}, bf16[128,128]{1,0:T(8,128)(2,1)S(1)}, u32[]{:S(2)}, u32[]{:S(2)}) collective-permute-start(bf16[128,128]{1,0:T(8,128)(2,1)S(1)} %get-tuple-element.39), channel_id=1, source_target_pairs={{2,4},{3,5},{6,8},{7,9},{10,12},{11,13},{14,16},{15,17},{18,20},{1... | collective-permute-start | bytes 98312 | tf_op jit(solution)/shard_map/ppermute | solution.py:399
  74.1 7.5 %collective-permute-start.15 = (bf16[128,128]{1,0:T(8,128)(2,1)S(1)}, bf16[128,128]{1,0:T(8,128)(2,1)S(1)}, u32[]{:S(2)}, u32[]{:S(2)}) collective-permute-start(bf16[128,128]{1,0:T(8,128)(2,1)S(1)} %get-tuple-element.39), channel_id=1, source_target_pairs={{3,4},{7,8},{11,12},{15,16},{19,20},{23,24},{27,28}} | collective-permute-start | bytes 98312 | tf_op jit(solution)/shard_map/ppermute | solution.py:399
  75.4 6.8 %collective-permute-start.16 = (bf16[128,128]{1,0:T(8,128)(2,1)S(1)}, bf16[128,128]{1,0:T(8,128)(2,1)S(1)}, u32[]{:S(2)}, u32[]{:S(2)}) collective-permute-start(bf16[128,128]{1,0:T(8,128)(2,1)S(1)} %get-tuple-element.40), channel_id=1, source_target_pairs={{2,0},{3,1},{6,4},{7,5},{10,8},{11,9},{14,12},{15,13},{18,16},{19,... | collective-permute-start | bytes 98312 | tf_op jit(solution)/shard_map/ppermute | solution.py:399
  76.7 7.7 %collective-permute-start.17 = (bf16[128,128]{1,0:T(8,128)(2,1)S(1)}, bf16[128,128]{1,0:T(8,128)(2,1)S(1)}, u32[]{:S(2)}, u32[]{:S(2)}) collective-permute-start(bf16[128,128]{1,0:T(8,128)(2,1)S(1)} %get-tuple-element.40), channel_id=1, source_target_pairs={{3,0},{7,4},{11,8},{15,12},{19,16},{23,20},{27,24},{31,28}} | collective-permute-start | bytes 98312 | tf_op jit(solution)/shard_map/ppermute | solution.py:399
where the time goes:
time: 86.4 us; the launch traced here: 85.8 us
  starting transfers between devices  32.5 us (38%)
  Pallas kernels  28.2 us (33%)
  waiting for transfers between devices  24.3 us (28%)
    ppermute x9, starting transfers between devices, gathered(): lax.ppermute(value, 'seq', [(i, i ^ k) for i in range(count)])  17.5 us
    ppermute x4, waiting for transfers between devices, swap(): return lax.ppermute(value, 'group', [(g, g ^ bits) for g in range(groups)])  11.1 us
    pallas_call x2, Pallas kernels, attend_rest(): pl.pallas_call(attend_rest_kernel, out_shape=jax.ShapeDtypeStruct((2 * sh...  10 us
    ppermute x5, starting transfers between devices, across(): return lax.ppermute(value, ('group', 'seq'), moves)  8.15 us
    ppermute x9, waiting for transfers between devices, gathered(): lax.ppermute(value, 'seq', [(i, i ^ k) for i in range(count)])  6.9 us
    ppermute x4, starting transfers between devices, swap(): return lax.ppermute(value, 'group', [(g, g ^ bits) for g in range(groups)])  6.78 us
    ppermute x5, waiting for transfers between devices, across(): return lax.ppermute(value, ('group', 'seq'), moves)  6.37 us
    pallas_call x2, Pallas kernels, attend_own(): pl.pallas_call(functools.partial(attend_own_kernel, count, window, own_wi...  6.36 us
  transfers between devices with their start and end apart: 18, of which 10 were waited for; matrix products, arithmetic and copies ran while one was open for 0% of the time, Pallas kernels for 23%

commit v1 on v0

--- a/solution.py
+++ b/solution.py
@@ -493,7 +493,9 @@
     second, *second_state = attend_own(1)
     first_rest = attend_rest(first_state)
     second_rest = attend_rest(second_state)
-    planes = [swap(own_part, bits) for bits in high[1:]]
+    planes = []
+    for bits in high[1:]:
+        planes.append(swap(own_part, bits))
     far = jnp.stack([own_part] + planes)
     near = swap(far, 1)
     scored = (
@@ -554,7 +556,8 @@
     deltas = list(range((total - OVMAX) // share, count))
     received = []
     for window, group_by in ((1, 1), (0, 0)):
-        received += [across(tails[window], group_by, [(i, i - d) for i in range(d, count)]) for d in deltas]
+        for d in deltas:
+            received.append(across(tails[window], group_by, [(i, i - d) for i in range(d, count)]))
     turned = pl.pallas_call(
         functools.partial(combine_kernel, count, deltas),
         out_shape=jax.ShapeDtypeStruct(turned.shape, F32),

time: 86.4 us -> 86.4 us (level)
  no operation moved by 1% of the time
where the time goes in v1:
time: 86.4 us; the launch traced here: 85.8 us
  starting transfers between devices  32.5 us (38%)
  Pallas kernels  28.2 us (33%)
  waiting for transfers between devices  24.3 us (28%)
    ppermute x9, starting transfers between devices, gathered(): lax.ppermute(value, 'seq', [(i, i ^ k) for i in range(count)])  17.5 us
    ppermute x4, waiting for transfers between devices, swap(): return lax.ppermute(value, 'group', [(g, g ^ bits) for g in range(groups)])  11.1 us
    pallas_call x2, Pallas kernels, attend_rest(): pl.pallas_call(attend_rest_kernel, out_shape=jax.ShapeDtypeStruct((2 * sh...  10 us
    ppermute x5, starting transfers between devices, across(): return lax.ppermute(value, ('group', 'seq'), moves)  8.15 us
    ppermute x9, waiting for transfers between devices, gathered(): lax.ppermute(value, 'seq', [(i, i ^ k) for i in range(count)])  6.9 us
    ppermute x4, starting transfers between devices, swap(): return lax.ppermute(value, 'group', [(g, g ^ bits) for g in range(groups)])  6.78 us
    ppermute x5, waiting for transfers between devices, across(): return lax.ppermute(value, ('group', 'seq'), moves)  6.37 us
    pallas_call x2, Pallas kernels, attend_own(): pl.pallas_call(functools.partial(attend_own_kernel, count, window, own_wi...  6.36 us
  transfers between devices with their start and end apart: 18, of which 10 were waited for; matrix products, arithmetic and copies ran while one was open for 0% of the time, Pallas kernels for 23%

profile of v1, /device:TPU:1, one launch (start us, length us, event | category | flops | bytes accessed | tf_op | source)
XLA Modules:
  0.0 85.8 jit_solution(16871966655698148716)
XLA Ops:
  0.0 4.2 %fold.1 = (bf16[256,128]{1,0:T(8,128)(2,1)S(1)}, bf16[256,1664]{1,0:T(8,128)(2,1)S(1)}, bf16[32,1664]{1,0:T(8,128)(2,1)S(1)}, bf16[128,1664]{1,0:T(8,128)(2,1)S(1)}, bf16[64,256]{1,0:T(8,128)(2,1)S(1)}) custom-call(bf16[64,1536]{1,0:T(8,128)(2,1)} %in_hbm.1, f32[1536]{0:T(1024)} %gain_hbm.1, bf16[3,1536,256]{2,1,0:T(8,128)(2,1)} %qkv_hbm.1, ...), custom_call_target="tpu_custom_call" | custom-call | flops 471859200 | bytes 3145728 | tf_op jit(solution)/shard_map/fold/pallas_call | solution.py:412
  4.2 2.2 %collective-permute-start.7 = (bf16[32,1664]{1,0:T(8,128)(2,1)S(1)}, bf16[32,1664]{1,0:T(8,128)(2,1)S(1)}, u32[]{:S(2)}, u32[]{:S(2)}) collective-permute-start(bf16[32,1664]{1,0:T(8,128)(2,1)S(1)} %get-tuple-element.33), channel_id=1, source_target_pairs={{0,1},{1,0},{2,3},{3,2},{4,5},{5,4},{6,7},{7,6},{8,9},{9,8},{10,11... | collective-permute-start | bytes 319496 | tf_op jit(solution)/shard_map/ppermute | solution.py:405
  6.4 2.3 %collective-permute-start.8 = (bf16[32,1664]{1,0:T(8,128)(2,1)S(1)}, bf16[32,1664]{1,0:T(8,128)(2,1)S(1)}, u32[]{:S(2)}, u32[]{:S(2)}) collective-permute-start(bf16[32,1664]{1,0:T(8,128)(2,1)S(1)} %get-tuple-element.33), channel_id=1, source_target_pairs={{0,2},{1,3},{2,0},{3,1},{4,6},{5,7},{6,4},{7,5},{8,10},{9,11},{10,... | collective-permute-start | bytes 319496 | tf_op jit(solution)/shard_map/ppermute | solution.py:405
  8.7 0.0 collective-permute-start.9
  8.7 0.4 collective-permute-done.7
  9.1 1.9 %collective-permute-done.8 = bf16[32,1664]{1,0:T(8,128)(2,1)S(1)} collective-permute-done((bf16[32,1664]{1,0:T(8,128)(2,1)S(1)}, bf16[32,1664]{1,0:T(8,128)(2,1)S(1)}, u32[]{:S(2)}, u32[]{:S(2)}) %collective-permute-start.8) | collective-permute-done | bytes 106528 | tf_op jit(solution)/shard_map/ppermute | solution.py:405
  11.0 4.6 %collective-permute-done.9 = bf16[32,1664]{1,0:T(8,128)(2,1)S(1)} collective-permute-done((bf16[32,1664]{1,0:T(8,128)(2,1)S(1)}, bf16[32,1664]{1,0:T(8,128)(2,1)S(1)}, u32[]{:S(2)}, u32[]{:S(2)}) %collective-permute-start.9) | collective-permute-done | bytes 106528 | tf_op jit(solution)/shard_map/ppermute | solution.py:405
  15.6 0.1 fusion
  15.6 1.2 %collective-permute-start.10 = (bf16[3,32,1664]{2,1,0:T(8,128)(2,1)S(1)}, bf16[3,32,1664]{2,1,0:T(8,128)(2,1)S(1)}, u32[]{:S(2)}, u32[]{:S(2)}) collective-permute-start(bf16[3,32,1664]{2,1,0:T(8,128)(2,1)S(1)} %get-tuple-element.42), channel_id=1, source_target_pairs={{0,8},{4,12},{8,0},{12,4},{16,24},{20,28},{24,16},{28,20},{1,9},{5... | collective-permute-start | bytes 958472 | tf_op jit(solution)/shard_map/ppermute | solution.py:402
  16.9 1.2 %collective-permute-start.11 = (bf16[3,32,1664]{2,1,0:T(8,128)(2,1)S(1)}, bf16[3,32,1664]{2,1,0:T(8,128)(2,1)S(1)}, u32[]{:S(2)}, u32[]{:S(2)}) collective-permute-start(bf16[3,32,1664]{2,1,0:T(8,128)(2,1)S(1)} %get-tuple-element.42), channel_id=1, source_target_pairs={{0,16},{4,20},{8,24},{12,28},{16,0},{20,4},{24,8},{28,12},{1,17},{... | collective-permute-start | bytes 958472 | tf_op jit(solution)/shard_map/ppermute | solution.py:402
  18.1 0.2 collective-permute-start.12
  18.4 0.1 copy.11
  18.5 0.1 copy.12
  18.6 3.4 %collective-permute-done.10 = bf16[3,32,1664]{2,1,0:T(8,128)(2,1)S(1)} collective-permute-done((bf16[3,32,1664]{2,1,0:T(8,128)(2,1)S(1)}, bf16[3,32,1664]{2,1,0:T(8,128)(2,1)S(1)}, u32[]{:S(2)}, u32[]{:S(2)}) %collective-permute-start.10) | collective-permute-done | bytes 319520 | tf_op jit(solution)/shard_map/ppermute | solution.py:402
  22.0 1.5 %collective-permute-done.11 = bf16[3,32,1664]{2,1,0:T(8,128)(2,1)S(1)} collective-permute-done((bf16[3,32,1664]{2,1,0:T(8,128)(2,1)S(1)}, bf16[3,32,1664]{2,1,0:T(8,128)(2,1)S(1)}, u32[]{:S(2)}, u32[]{:S(2)}) %collective-permute-start.11) | collective-permute-done | bytes 319520 | tf_op jit(solution)/shard_map/ppermute | solution.py:402
  23.5 6.2 %collective-permute-done.12 = bf16[3,32,1664]{2,1,0:T(8,128)(2,1)S(1)} collective-permute-done((bf16[3,32,1664]{2,1,0:T(8,128)(2,1)S(1)}, bf16[3,32,1664]{2,1,0:T(8,128)(2,1)S(1)}, u32[]{:S(2)}, u32[]{:S(2)}) %collective-permute-start.12) | collective-permute-done | bytes 319520 | tf_op jit(solution)/shard_map/ppermute | solution.py:402
  29.7 0.2 pad_maximum_fusion.refs_6_
  29.9 4.1 %collective-permute-start.13 = (bf16[4,3,32,1664]{3,2,1,0:T(8,128)(2,1)S(1)}, bf16[4,3,32,1664]{3,2,1,0:T(8,128)(2,1)S(1)}, u32[]{:S(2)}, u32[]{:S(2)}) collective-permute-start(bf16[4,3,32,1664]{3,2,1,0:T(8,128)(2,1)S(1)} %pad_maximum_fusion.refs_6_), channel_id=1, source_target_pairs={{0,4},{4,0},{8,12},{12,8},{16,20},{20,16},{24,28},{28,24},{1,5},{5... | collective-permute-start | bytes 3833864 | tf_op jit(solution)/shard_map/ppermute | solution.py:402
  34.0 0.1 pad_maximum_fusion.3.refs_0_
  34.1 2.5 %collective-permute-start = (bf16[256,128]{1,0:T(8,128)(2,1)S(1)}, bf16[256,128]{1,0:T(8,128)(2,1)S(1)}, u32[]{:S(2)}, u32[]{:S(2)}) collective-permute-start(bf16[256,128]{1,0:T(8,128)(2,1)S(1)} %pad_maximum_fusion.3.refs_0_), channel_id=1, source_target_pairs={{0,1},{1,0},{2,3},{3,2},{4,5},{5,4},{6,7},{7,6},{8,9},{9,8},{10,11... | collective-permute-start | bytes 196616 | tf_op jit(solution)/shard_map/ppermute | solution.py:405
  36.5 1.5 %collective-permute-start.1 = (bf16[256,128]{1,0:T(8,128)(2,1)S(1)}, bf16[256,128]{1,0:T(8,128)(2,1)S(1)}, u32[]{:S(2)}, u32[]{:S(2)}) collective-permute-start(bf16[256,128]{1,0:T(8,128)(2,1)S(1)} %pad_maximum_fusion.3.refs_0_), channel_id=1, source_target_pairs={{0,2},{1,3},{2,0},{3,1},{4,6},{5,7},{6,4},{7,5},{8,10},{9,11},{10,... | collective-permute-start | bytes 196616 | tf_op jit(solution)/shard_map/ppermute | solution.py:405
  38.0 1.1 %collective-permute-start.2 = (bf16[256,128]{1,0:T(8,128)(2,1)S(1)}, bf16[256,128]{1,0:T(8,128)(2,1)S(1)}, u32[]{:S(2)}, u32[]{:S(2)}) collective-permute-start(bf16[256,128]{1,0:T(8,128)(2,1)S(1)} %pad_maximum_fusion.3.refs_0_), channel_id=1, source_target_pairs={{0,3},{1,2},{2,1},{3,0},{4,7},{5,6},{6,5},{7,4},{8,11},{9,10},{10,... | collective-permute-start | bytes 196616 | tf_op jit(solution)/shard_map/ppermute | solution.py:405
  39.1 0.3 collective-permute-start.3
  39.4 0.0 collective-permute-done.refs_1_
  39.4 2.2 %collective-permute-start.4 = (bf16[256,128]{1,0:T(8,128)(2,1)S(1)}, bf16[256,128]{1,0:T(8,128)(2,1)S(1)}, u32[]{:S(2)}, u32[]{:S(2)}) collective-permute-start(bf16[256,128]{1,0:T(8,128)(2,1)S(1)} %get-tuple-element.24.refs_4_), channel_id=1, source_target_pairs={{0,2},{1,3},{2,0},{3,1},{4,6},{5,7},{6,4},{7,5},{8,10},{9,11},{10,... | collective-permute-start | bytes 196616 | tf_op jit(solution)/shard_map/ppermute | solution.py:405
  41.6 0.0 collective-permute-done.1.refs_2_
  41.6 5.5 %collective-permute-start.5 = (bf16[256,128]{1,0:T(8,128)(2,1)S(1)}, bf16[256,128]{1,0:T(8,128)(2,1)S(1)}, u32[]{:S(2)}, u32[]{:S(2)}) collective-permute-start(bf16[256,128]{1,0:T(8,128)(2,1)S(1)} %get-tuple-element.24.refs_4_), channel_id=1, source_target_pairs={{0,3},{1,2},{2,1},{3,0},{4,7},{5,6},{6,5},{7,4},{8,11},{9,10},{10,... | collective-permute-start | bytes 196616 | tf_op jit(solution)/shard_map/ppermute | solution.py:405
  47.1 0.0 collective-permute-done.2.refs_3_
  47.1 0.1 pad_maximum_fusion.2
  47.2 3.0 %collective-permute-start.6 = (bf16[4,256,128]{2,1,0:T(8,128)(2,1)S(1)}, bf16[4,256,128]{2,1,0:T(8,128)(2,1)S(1)}, u32[]{:S(2)}, u32[]{:S(2)}) collective-permute-start(bf16[4,256,128]{2,1,0:T(8,128)(2,1)S(1)} %pad_maximum_fusion.2), channel_id=1, source_target_pairs={{4,0},{5,1},{6,2},{7,3},{8,4},{9,5},{10,6},{11,7},{12,8},{13,9},{1... | collective-permute-start | bytes 786440 | tf_op jit(solution)/shard_map/ppermute | solution.py:399
  50.2 3.2 %attend_own.2 = (bf16[512,384]{1,0:T(8,128)(2,1)S(1)}, bf16[1024,128]{1,0:T(8,128)(2,1)S(1)}, bf16[256,128]{1,0:T(8,128)(2,1)S(1)}, bf16[1024,256]{1,0:T(8,128)(2,1)S(1)}, f32[8,1024]{1,0:T(8,128)S(1)}) custom-call(s32[15]{0:T(128)S(1)} %copy-done.1, bf16[256,128]{1,0:T(8,128)(2,1)S(1)} %pad_maximum_fusion.3.refs_0_, ...), custom_call_target="tpu_custom_call" | custom-call | flops 1073741824 | bytes 262144 | tf_op jit(solution)/shard_map/attend_own/pallas_call | solution.py:458
  53.4 0.0 collective-permute-done.3.refs_0_
  53.4 0.0 collective-permute-done.5.refs_2_
  53.4 4.9 %attend_rest.2.refs_1_.refs_0_ = bf16[512,768]{1,0:T(8,128)(2,1)S(1)} custom-call(bf16[64,256]{1,0:T(8,128)(2,1)S(1)} %get-tuple-element.23.refs_5_.gram_ref, bf16[1024,128]{1,0:T(8,128)(2,1)S(1)} %get-tuple-element.25.right_ref, bf16[256,128]{1,0:T(8,128)(2,1)S(1)} %get-tuple-element.26.mine_ref, bf16[1024,256]{1,0:T(8,128)(2,1)S(1)} %get-tuple-element.27.ext_ref, ...), custom_call_target="tpu_custom_call" | custom-call | flops 3221225472 | bytes 786432 | tf_op jit(solution)/shard_map/attend_rest/pallas_call | solution.py:481
  58.3 0.0 collective-permute-done.6.refs_6_
  58.3 3.2 %attend_own.3 = (bf16[512,384]{1,0:T(8,128)(2,1)S(1)}, bf16[1024,128]{1,0:T(8,128)(2,1)S(1)}, bf16[256,128]{1,0:T(8,128)(2,1)S(1)}, bf16[1024,256]{1,0:T(8,128)(2,1)S(1)}, f32[8,1024]{1,0:T(8,128)S(1)}) custom-call(s32[15]{0:T(128)S(1)} %copy-done.1, bf16[256,128]{1,0:T(8,128)(2,1)S(1)} %pad_maximum_fusion.3.refs_0_, ...), custom_call_target="tpu_custom_call" | custom-call | flops 1073741824 | bytes 262144 | tf_op jit(solution)/shard_map/attend_own/pallas_call | solution.py:458
  61.5 5.1 %attend_rest.3.refs_3_.refs_1_ = bf16[512,768]{1,0:T(8,128)(2,1)S(1)} custom-call(bf16[64,256]{1,0:T(8,128)(2,1)S(1)} %get-tuple-element.23.refs_5_.gram_ref, bf16[1024,128]{1,0:T(8,128)(2,1)S(1)} %get-tuple-element.29.right_ref, bf16[256,128]{1,0:T(8,128)(2,1)S(1)} %get-tuple-element.30.mine_ref, bf16[1024,256]{1,0:T(8,128)(2,1)S(1)} %get-tuple-element.31.ext_ref, ...), custom_call_target="tpu_custom_call" | custom-call | flops 3221225472 | bytes 786432 | tf_op jit(solution)/shard_map/attend_rest/pallas_call | solution.py:481
  66.7 3.2 %finish_far.1.refs_3_ = f32[1024,1664]{1,0:T(8,128)S(1)} custom-call(bf16[512,384]{1,0:T(8,128)(2,1)S(1)} %get-tuple-element.34.refs_0_, bf16[512,768]{1,0:T(8,128)(2,1)S(1)} %attend_rest.2.refs_1_.refs_0_, bf16[512,384]{1,0:T(8,128)(2,1)S(1)} %get-tuple-element.35.refs_2_, bf16[512,768]{1,0:T(8,128)(2,1)S(1)} %attend_rest.3.refs_3_.refs_1_, ...), custom_call_target="tpu_custom_call" | custom-call | flops 2617245696 | bytes 5111808 | tf_op jit(solution)/shard_map/finish_far/pallas_call | solution.py:511
  69.9 2.9 %finish_near.1 = (f32[2,256,128]{2,1,0:T(8,128)S(1)}, bf16[128,128]{1,0:T(8,128)(2,1)S(1)}, bf16[128,128]{1,0:T(8,128)(2,1)S(1)}) custom-call(s32[15]{0:T(128)S(1)} %copy-done.1, bf16[512,768]{1,0:T(8,128)(2,1)S(1)} %attend_rest.2.refs_1_.refs_0_, bf16[512,768]{1,0:T(8,128)(2,1)S(1)} %attend_rest.3.refs_3_.refs_1_, ...), custom_call_target="tpu_custom_call" | custom-call | flops 1308622848 | bytes 2555904 | tf_op jit(solution)/shard_map/finish_near/pallas_call | solution.py:523
  72.8 1.3 %collective-permute-start.14 = (bf16[128,128]{1,0:T(8,128)(2,1)S(1)}, bf16[128,128]{1,0:T(8,128)(2,1)S(1)}, u32[]{:S(2)}, u32[]{:S(2)}) collective-permute-start(bf16[128,128]{1,0:T(8,128)(2,1)S(1)} %get-tuple-element.39), channel_id=1, source_target_pairs={{2,4},{3,5},{6,8},{7,9},{10,12},{11,13},{14,16},{15,17},{18,20},{1... | collective-permute-start | bytes 98312 | tf_op jit(solution)/shard_map/ppermute | solution.py:399
  74.1 1.3 %collective-permute-start.15 = (bf16[128,128]{1,0:T(8,128)(2,1)S(1)}, bf16[128,128]{1,0:T(8,128)(2,1)S(1)}, u32[]{:S(2)}, u32[]{:S(2)}) collective-permute-start(bf16[128,128]{1,0:T(8,128)(2,1)S(1)} %get-tuple-element.39), channel_id=1, source_target_pairs={{3,4},{7,8},{11,12},{15,16},{19,20},{23,24},{27,28}} | collective-permute-start | bytes 98312 | tf_op jit(solution)/shard_map/ppermute | solution.py:399
  75.4 1.3 %collective-permute-start.16 = (bf16[128,128]{1,0:T(8,128)(2,1)S(1)}, bf16[128,128]{1,0:T(8,128)(2,1)S(1)}, u32[]{:S(2)}, u32[]{:S(2)}) collective-permute-start(bf16[128,128]{1,0:T(8,128)(2,1)S(1)} %get-tuple-element.40), channel_id=1, source_target_pairs={{2,0},{3,1},{6,4},{7,5},{10,8},{11,9},{14,12},{15,13},{18,16},{19,... | collective-permute-start | bytes 98312 | tf_op jit(solution)/shard_map/ppermute | solution.py:399
  76.7 1.3 %collective-permute-start.17 = (bf16[128,128]{1,0:T(8,128)(2,1)S(1)}, bf16[128,128]{1,0:T(8,128)(2,1)S(1)}, u32[]{:S(2)}, u32[]{:S(2)}) collective-permute-start(bf16[128,128]{1,0:T(8,128)(2,1)S(1)} %get-tuple-element.40), channel_id=1, source_target_pairs={{3,0},{7,4},{11,8},{15,12},{19,16},{23,20},{27,24},{31,28}} | collective-permute-start | bytes 98312 | tf_op jit(solution)/shard_map/ppermute | solution.py:399
  78.0 1.3 %collective-permute-done.14.refs_0_ = bf16[128,128]{1,0:T(8,128)(2,1)S(1)} collective-permute-done((bf16[128,128]{1,0:T(8,128)(2,1)S(1)}, bf16[128,128]{1,0:T(8,128)(2,1)S(1)}, u32[]{:S(2)}, u32[]{:S(2)}) %collective-permute-start.14) | collective-permute-done | bytes 32800 | tf_op jit(solution)/shard_map/ppermute | solution.py:399
  79.3 2.3 %collective-permute-done.15.refs_1_ = bf16[128,128]{1,0:T(8,128)(2,1)S(1)} collective-permute-done((bf16[128,128]{1,0:T(8,128)(2,1)S(1)}, bf16[128,128]{1,0:T(8,128)(2,1)S(1)}, u32[]{:S(2)}, u32[]{:S(2)}) %collective-permute-start.15) | collective-permute-done | bytes 32800 | tf_op jit(solution)/shard_map/ppermute | solution.py:399
  81.6 0.6 collective-permute-done.16.refs_2_
  82.2 2.2 %collective-permute-done.17.refs_3_ = bf16[128,128]{1,0:T(8,128)(2,1)S(1)} collective-permute-done((bf16[128,128]{1,0:T(8,128)(2,1)S(1)}, bf16[128,128]{1,0:T(8,128)(2,1)S(1)}, u32[]{:S(2)}, u32[]{:S(2)}) %collective-permute-start.17) | collective-permute-done | bytes 32800 | tf_op jit(solution)/shard_map/ppermute | solution.py:399
  84.4 1.5 %combine.1 = f32[2,64,256]{2,1,0:T(8,128)} custom-call(s32[15]{0:T(128)S(1)} %copy-done.1, f32[2,64,256]{2,1,0:T(8,128)S(1)} %bitcast.16, f32[2,256,128]{2,1,0:T(8,128)S(1)} %get-tuple-element.38.rows_ref, bf16[128,128]{1,0:T(8,128)(2,1)S(1)} %collective-permute-done.14.refs_0_, bf16[128,128]{1,0:T(8,128)(2,1)S(1)} %collective-permute-done.15.refs_1_, ...), custom_call_target="tpu_custom_call" | custom-call | tf_op jit(solution)/shard_map/combine/pallas_call | solution.py:561
  (7 shorter events, 0.0 us)
Async XLA Ops:
  0.0 18.4 %copy-start = (f32[2,256,64]{1,2,0:T(8,128)S(1)}, f32[2,256,64]{1,2,0:T(8,128)}, u32[]{:S(2)}) copy-start(f32[2,256,64]{1,2,0:T(8,128)} %param.8) | copy-start | bytes 393220
  4.2 4.9 %collective-permute-start.7 = (bf16[32,1664]{1,0:T(8,128)(2,1)S(1)}, bf16[32,1664]{1,0:T(8,128)(2,1)S(1)}, u32[]{:S(2)}, u32[]{:S(2)}) collective-permute-start(bf16[32,1664]{1,0:T(8,128)(2,1)S(1)} %get-tuple-element.33), channel_id=1, source_target_pairs={{0,1},{1,0},{2,3},{3,2},{4,5},{5,4},{6,7},{7,6},{8,9},{9,8},{10,11... | collective-permute-start | bytes 319496 | tf_op jit(solution)/shard_map/ppermute | solution.py:405
  6.4 4.6 %collective-permute-start.8 = (bf16[32,1664]{1,0:T(8,128)(2,1)S(1)}, bf16[32,1664]{1,0:T(8,128)(2,1)S(1)}, u32[]{:S(2)}, u32[]{:S(2)}) collective-permute-start(bf16[32,1664]{1,0:T(8,128)(2,1)S(1)} %get-tuple-element.33), channel_id=1, source_target_pairs={{0,2},{1,3},{2,0},{3,1},{4,6},{5,7},{6,4},{7,5},{8,10},{9,11},{10,... | collective-permute-start | bytes 319496 | tf_op jit(solution)/shard_map/ppermute | solution.py:405
  8.7 6.9 %collective-permute-start.9 = (bf16[32,1664]{1,0:T(8,128)(2,1)S(1)}, bf16[32,1664]{1,0:T(8,128)(2,1)S(1)}, u32[]{:S(2)}, u32[]{:S(2)}) collective-permute-start(bf16[32,1664]{1,0:T(8,128)(2,1)S(1)} %get-tuple-element.33), channel_id=1, source_target_pairs={{0,3},{1,2},{2,1},{3,0},{4,7},{5,6},{6,5},{7,4},{8,11},{9,10},{10,... | collective-permute-start | bytes 319496 | tf_op jit(solution)/shard_map/ppermute | solution.py:405
  15.6 6.4 %collective-permute-start.10 = (bf16[3,32,1664]{2,1,0:T(8,128)(2,1)S(1)}, bf16[3,32,1664]{2,1,0:T(8,128)(2,1)S(1)}, u32[]{:S(2)}, u32[]{:S(2)}) collective-permute-start(bf16[3,32,1664]{2,1,0:T(8,128)(2,1)S(1)} %get-tuple-element.42), channel_id=1, source_target_pairs={{0,8},{4,12},{8,0},{12,4},{16,24},{20,28},{24,16},{28,20},{1,9},{5... | collective-permute-start | bytes 958472 | tf_op jit(solution)/shard_map/ppermute | solution.py:402
  16.9 6.6 %collective-permute-start.11 = (bf16[3,32,1664]{2,1,0:T(8,128)(2,1)S(1)}, bf16[3,32,1664]{2,1,0:T(8,128)(2,1)S(1)}, u32[]{:S(2)}, u32[]{:S(2)}) collective-permute-start(bf16[3,32,1664]{2,1,0:T(8,128)(2,1)S(1)} %get-tuple-element.42), channel_id=1, source_target_pairs={{0,16},{4,20},{8,24},{12,28},{16,0},{20,4},{24,8},{28,12},{1,17},{... | collective-permute-start | bytes 958472 | tf_op jit(solution)/shard_map/ppermute | solution.py:402
  18.1 11.6 %collective-permute-start.12 = (bf16[3,32,1664]{2,1,0:T(8,128)(2,1)S(1)}, bf16[3,32,1664]{2,1,0:T(8,128)(2,1)S(1)}, u32[]{:S(2)}, u32[]{:S(2)}) collective-permute-start(bf16[3,32,1664]{2,1,0:T(8,128)(2,1)S(1)} %get-tuple-element.42), channel_id=1, source_target_pairs={{0,24},{4,28},{8,16},{12,20},{16,8},{20,12},{24,0},{28,4},{1,25},{... | collective-permute-start | bytes 958472 | tf_op jit(solution)/shard_map/ppermute | solution.py:402
  29.7 20.5 %copy-start.1 = (s32[15]{0:T(128)S(1)}, s32[15]{0:T(128)}, u32[]{:S(2)}) copy-start(s32[15]{0:T(128)} %margin_ref.7) | copy-start | bytes 184
  29.9 40.0 %collective-permute-start.13 = (bf16[4,3,32,1664]{3,2,1,0:T(8,128)(2,1)S(1)}, bf16[4,3,32,1664]{3,2,1,0:T(8,128)(2,1)S(1)}, u32[]{:S(2)}, u32[]{:S(2)}) collective-permute-start(bf16[4,3,32,1664]{3,2,1,0:T(8,128)(2,1)S(1)} %pad_maximum_fusion.refs_6_), channel_id=1, source_target_pairs={{0,4},{4,0},{8,12},{12,8},{16,20},{20,16},{24,28},{28,24},{1,5},{5... | collective-permute-start | bytes 3833864 | tf_op jit(solution)/shard_map/ppermute | solution.py:402
  34.1 5.4 %collective-permute-start = (bf16[256,128]{1,0:T(8,128)(2,1)S(1)}, bf16[256,128]{1,0:T(8,128)(2,1)S(1)}, u32[]{:S(2)}, u32[]{:S(2)}) collective-permute-start(bf16[256,128]{1,0:T(8,128)(2,1)S(1)} %pad_maximum_fusion.3.refs_0_), channel_id=1, source_target_pairs={{0,1},{1,0},{2,3},{3,2},{4,5},{5,4},{6,7},{7,6},{8,9},{9,8},{10,11... | collective-permute-start | bytes 196616 | tf_op jit(solution)/shard_map/ppermute | solution.py:405
  36.5 5.1 %collective-permute-start.1 = (bf16[256,128]{1,0:T(8,128)(2,1)S(1)}, bf16[256,128]{1,0:T(8,128)(2,1)S(1)}, u32[]{:S(2)}, u32[]{:S(2)}) collective-permute-start(bf16[256,128]{1,0:T(8,128)(2,1)S(1)} %pad_maximum_fusion.3.refs_0_), channel_id=1, source_target_pairs={{0,2},{1,3},{2,0},{3,1},{4,6},{5,7},{6,4},{7,5},{8,10},{9,11},{10,... | collective-permute-start | bytes 196616 | tf_op jit(solution)/shard_map/ppermute | solution.py:405
  38.0 9.1 %collective-permute-start.2 = (bf16[256,128]{1,0:T(8,128)(2,1)S(1)}, bf16[256,128]{1,0:T(8,128)(2,1)S(1)}, u32[]{:S(2)}, u32[]{:S(2)}) collective-permute-start(bf16[256,128]{1,0:T(8,128)(2,1)S(1)} %pad_maximum_fusion.3.refs_0_), channel_id=1, source_target_pairs={{0,3},{1,2},{2,1},{3,0},{4,7},{5,6},{6,5},{7,4},{8,11},{9,10},{10,... | collective-permute-start | bytes 196616 | tf_op jit(solution)/shard_map/ppermute | solution.py:405
  39.1 14.2 %collective-permute-start.3 = (bf16[256,128]{1,0:T(8,128)(2,1)S(1)}, bf16[256,128]{1,0:T(8,128)(2,1)S(1)}, u32[]{:S(2)}, u32[]{:S(2)}) collective-permute-start(bf16[256,128]{1,0:T(8,128)(2,1)S(1)} %get-tuple-element.24.refs_4_), channel_id=1, source_target_pairs={{0,1},{1,0},{2,3},{3,2},{4,5},{5,4},{6,7},{7,6},{8,9},{9,8},{10,11... | collective-permute-start | bytes 196616 | tf_op jit(solution)/shard_map/ppermute | solution.py:405
  39.4 14.0 %collective-permute-start.4 = (bf16[256,128]{1,0:T(8,128)(2,1)S(1)}, bf16[256,128]{1,0:T(8,128)(2,1)S(1)}, u32[]{:S(2)}, u32[]{:S(2)}) collective-permute-start(bf16[256,128]{1,0:T(8,128)(2,1)S(1)} %get-tuple-element.24.refs_4_), channel_id=1, source_target_pairs={{0,2},{1,3},{2,0},{3,1},{4,6},{5,7},{6,4},{7,5},{8,10},{9,11},{10,... | collective-permute-start | bytes 196616 | tf_op jit(solution)/shard_map/ppermute | solution.py:405
  41.6 11.8 %collective-permute-start.5 = (bf16[256,128]{1,0:T(8,128)(2,1)S(1)}, bf16[256,128]{1,0:T(8,128)(2,1)S(1)}, u32[]{:S(2)}, u32[]{:S(2)}) collective-permute-start(bf16[256,128]{1,0:T(8,128)(2,1)S(1)} %get-tuple-element.24.refs_4_), channel_id=1, source_target_pairs={{0,3},{1,2},{2,1},{3,0},{4,7},{5,6},{6,5},{7,4},{8,11},{9,10},{10,... | collective-permute-start | bytes 196616 | tf_op jit(solution)/shard_map/ppermute | solution.py:405
  47.2 11.1 %collective-permute-start.6 = (bf16[4,256,128]{2,1,0:T(8,128)(2,1)S(1)}, bf16[4,256,128]{2,1,0:T(8,128)(2,1)S(1)}, u32[]{:S(2)}, u32[]{:S(2)}) collective-permute-start(bf16[4,256,128]{2,1,0:T(8,128)(2,1)S(1)} %pad_maximum_fusion.2), channel_id=1, source_target_pairs={{4,0},{5,1},{6,2},{7,3},{8,4},{9,5},{10,6},{11,7},{12,8},{13,9},{1... | collective-permute-start | bytes 786440 | tf_op jit(solution)/shard_map/ppermute | solution.py:399
  72.8 6.5 %collective-permute-start.14 = (bf16[128,128]{1,0:T(8,128)(2,1)S(1)}, bf16[128,128]{1,0:T(8,128)(2,1)S(1)}, u32[]{:S(2)}, u32[]{:S(2)}) collective-permute-start(bf16[128,128]{1,0:T(8,128)(2,1)S(1)} %get-tuple-element.39), channel_id=1, source_target_pairs={{2,4},{3,5},{6,8},{7,9},{10,12},{11,13},{14,16},{15,17},{18,20},{1... | collective-permute-start | bytes 98312 | tf_op jit(solution)/shard_map/ppermute | solution.py:399
  74.1 7.5 %collective-permute-start.15 = (bf16[128,128]{1,0:T(8,128)(2,1)S(1)}, bf16[128,128]{1,0:T(8,128)(2,1)S(1)}, u32[]{:S(2)}, u32[]{:S(2)}) collective-permute-start(bf16[128,128]{1,0:T(8,128)(2,1)S(1)} %get-tuple-element.39), channel_id=1, source_target_pairs={{3,4},{7,8},{11,12},{15,16},{19,20},{23,24},{27,28}} | collective-permute-start | bytes 98312 | tf_op jit(solution)/shard_map/ppermute | solution.py:399
  75.4 6.8 %collective-permute-start.16 = (bf16[128,128]{1,0:T(8,128)(2,1)S(1)}, bf16[128,128]{1,0:T(8,128)(2,1)S(1)}, u32[]{:S(2)}, u32[]{:S(2)}) collective-permute-start(bf16[128,128]{1,0:T(8,128)(2,1)S(1)} %get-tuple-element.40), channel_id=1, source_target_pairs={{2,0},{3,1},{6,4},{7,5},{10,8},{11,9},{14,12},{15,13},{18,16},{19,... | collective-permute-start | bytes 98312 | tf_op jit(solution)/shard_map/ppermute | solution.py:399
  76.7 7.7 %collective-permute-start.17 = (bf16[128,128]{1,0:T(8,128)(2,1)S(1)}, bf16[128,128]{1,0:T(8,128)(2,1)S(1)}, u32[]{:S(2)}, u32[]{:S(2)}) collective-permute-start(bf16[128,128]{1,0:T(8,128)(2,1)S(1)} %get-tuple-element.40), channel_id=1, source_target_pairs={{3,0},{7,4},{11,8},{15,12},{19,16},{23,20},{27,24},{31,28}} | collective-permute-start | bytes 98312 | tf_op jit(solution)/shard_map/ppermute | solution.py:399
